TPU v7x, 32 devices: a whole 2x2x4 slice. The times are simulated.
32 devices in a mesh: team: 2 (over x), blk: 4 (over z), head: 4 (over y, core).
Axes of the slice: x: 2, y: 2, z: 4, core: 2. Of those that a mesh axis runs over, the one named last changes fastest.
Arguments:
- queries: bfloat16 [1024, 8, 8, 128], P('blk', 'head', 'team'), may hold values from -40 to 40
- features: bfloat16 [1024, 8192], P('blk', ('team', 'head')), may hold values from -6 to 6
- adapter_down: bfloat16 [4, 8192, 64], P(None, ('team', 'head')), may hold values from -0.0625 to 0.0625
- adapter_key_up: bfloat16 [4, 64, 8, 128], P(None, None, 'head'), may hold values from -0.75 to 0.75
- adapter_value_up: bfloat16 [4, 64, 8, 128], P(None, None, 'head'), may hold values from -0.75 to 0.75
- base_key: bfloat16 [1024, 8, 128], P('blk', 'head'), may hold values from -6 to 6
- base_value: bfloat16 [1024, 8, 128], P('blk', 'head'), may hold values from -24 to 24
- prefix_key: bfloat16 [2048, 8, 128], P('blk', 'head'), may hold values from -7 to 7
- prefix_value: bfloat16 [2048, 8, 128], P('blk', 'head'), may hold values from -24 to 24
- adapter_ids: int32 [4], replicated, may hold values from 0 to 3
- block_order: int32 [4], replicated, may hold values from 0 to 15
Outputs:
- attended: bfloat16 [1024, 8, 8, 128], P('blk', 'head', 'team')
All inputs are finite; a program needn't handle non-finite values.
Results may differ from a plain program's by a relative error of at most 0.011.
Values may be sent and summed in bfloat16 or wider, within the bound.
No kernel may reach another device: no remote copies, remote signals or barrier semaphores. Data moves between devices by JAX's collectives and lax.ppermute only.
A program may use at most 64 MiB of HBM per device.

v0:
```python
import math
import jax
import jax.numpy as jnp
from jax import lax
from jax.sharding import PartitionSpec as P

NEG_FILL = -1e30


def block_length(row_count):
    for candidate in range(min(row_count, 1024), 0, -1):
        if row_count % candidate == 0:
            return candidate
    return row_count


def key_positions(row_count, shard_rows, prefix_dev, query_dev, block_order, block_count):
    row_index = jnp.arange(row_count, dtype=jnp.int32)
    holder = row_index // shard_rows
    within = row_index - holder * shard_rows
    block_ids = jnp.arange(block_count, dtype=jnp.int32)
    holder_order = jnp.sum(
        jnp.where(holder[:, None] == block_ids[None, :], block_order[None, :], 0), axis=1
    )
    later = prefix_dev * block_count + holder_order * query_dev + within - prefix_dev
    return jnp.where(within < prefix_dev, holder * prefix_dev + within, later)


def attend(running, query_rows, query_pos, key_rows, value_rows, key_pos):
    row_count = key_rows.shape[0]
    block_rows = block_length(row_count)
    key_blocks = row_count // block_rows
    kv_heads = key_rows.shape[1]
    head_dim = key_rows.shape[2]
    score_scale = 1.0 / math.sqrt(head_dim)
    latest = jnp.max(query_pos)
    key_split = key_rows.reshape((key_blocks, block_rows, kv_heads, head_dim))
    value_split = value_rows.reshape((key_blocks, block_rows, kv_heads, head_dim))
    pos_split = key_pos.reshape((key_blocks, block_rows))

    def advance(carried, block_data):
        block_keys, block_values, block_pos = block_data

        def compute(previous):
            row_max, row_sum, weighted = previous
            scores = (
                jnp.einsum(
                    "tkgd,skd->kgts", query_rows, block_keys, preferred_element_type=jnp.float32
                )
                * score_scale
            )
            visible = block_pos[None, None, None, :] <= query_pos[None, None, :, None]
            scores = jnp.where(visible, scores, NEG_FILL)
            new_max = jnp.maximum(row_max, jnp.max(scores, axis=-1))
            weights = jnp.where(visible, jnp.exp(scores - new_max[..., None]), 0.0)
            factor = jnp.exp(row_max - new_max)
            row_sum = row_sum * factor + jnp.sum(weights, axis=-1)
            product = jnp.einsum(
                "kgts,skd->kgtd",
                weights.astype(jnp.bfloat16),
                block_values,
                preferred_element_type=jnp.float32,
            )
            weighted = weighted * factor[..., None] + product
            return (new_max, row_sum, weighted)

        return (lax.cond(jnp.min(block_pos) > latest, lambda kept: kept, compute, carried), None)

    result, _ = lax.scan(advance, running, (key_split, value_split, pos_split))
    return result


def on_device(
    queries,
    features,
    adapter_down,
    adapter_key_up,
    adapter_value_up,
    base_key,
    base_value,
    prefix_key,
    prefix_value,
    adapter_ids,
    block_order,
):
    block_count = lax.axis_size("blk")
    my_block = lax.axis_index("blk")
    query_dev = queries.shape[0]
    kv_heads = queries.shape[1]
    group_dev = queries.shape[2]
    head_dim = queries.shape[3]
    prefix_dev = prefix_key.shape[0]
    rank_width = adapter_down.shape[2]
    shard_rows = prefix_dev + query_dev
    chosen = adapter_ids[my_block]
    down_rows = lax.dynamic_index_in_dim(adapter_down, chosen, 0, keepdims=False)
    partial_latent = jnp.dot(features, down_rows, preferred_element_type=jnp.float32)
    latent = lax.psum(partial_latent, ("team", "head")).astype(jnp.bfloat16)

    def expand(up_table, base_rows):
        up_rows = lax.dynamic_index_in_dim(up_table, chosen, 0, keepdims=False).reshape(
            rank_width, kv_heads * head_dim
        )
        delta = jnp.dot(latent, up_rows, preferred_element_type=jnp.float32).reshape(
            query_dev, kv_heads, head_dim
        )
        return (base_rows.astype(jnp.float32) + delta).astype(jnp.bfloat16)

    key_rows = jnp.concatenate([prefix_key, expand(adapter_key_up, base_key)], axis=0)
    value_rows = jnp.concatenate([prefix_value, expand(adapter_value_up, base_value)], axis=0)
    prefix_total = prefix_dev * block_count
    offsets = jnp.arange(query_dev, dtype=jnp.int32)
    query_pos = prefix_total + block_order[my_block] * query_dev + offsets
    initial = (
        jnp.full((kv_heads, group_dev, query_dev), NEG_FILL, jnp.float32),
        jnp.zeros((kv_heads, group_dev, query_dev), jnp.float32),
        jnp.zeros((kv_heads, group_dev, query_dev, head_dim), jnp.float32),
    )
    key_piece = lax.all_gather(key_rows, "blk", axis=0, tiled=True)
    value_piece = lax.all_gather(value_rows, "blk", axis=0, tiled=True)
    piece_pos = key_positions(
        key_piece.shape[0], shard_rows, prefix_dev, query_dev, block_order, block_count
    )
    row_max, row_sum, weighted = attend(
        initial, queries, query_pos, key_piece, value_piece, piece_pos
    )
    result = weighted / row_sum[..., None]
    return result.transpose(2, 0, 1, 3).astype(jnp.bfloat16)


def solution(mesh):
    placed = (
        P("blk", "head", "team", None),
        P("blk", ("team", "head")),
        P(None, ("team", "head"), None),
        P(None, None, "head", None),
        P(None, None, "head", None),
        P("blk", "head", None),
        P("blk", "head", None),
        P("blk", "head", None),
        P("blk", "head", None),
        P(),
        P(),
    )
    return jax.shard_map(
        on_device,
        mesh=mesh,
        in_specs=placed,
        out_specs=P("blk", "head", "team", None),
        check_vma=False,
    )
```

profile of v0, /device:TPU:0, one launch (start us, length us, event | category | flops | bytes accessed | tf_op | source)
XLA Modules:
  0.0 160.4 jit_solution(10820601032562232662)
XLA Ops:
  6.5 0.0 copy-start
  6.5 0.0 all-gather.3.cloned.1.call-start
  6.5 1.3 dynamic_slice.39
  9.8 0.0 copy-done
  9.8 1.2 convolution_bitcast_fusion
  11.0 26.0 %psum.7 = bf16[256,64]{0,1:T(8,128)(2,1)S(1)} all-reduce(f32[256,64]{0,1:T(8,128)S(1)} %convolution_bitcast_fusion), channel_id=1, replica_groups=mesh['team'=2,'blk'=4,'head'=4] {'team','head'}, use_global_device_ids=true, to_apply=%region_0.1 | all-reduce | flops 16384 | bytes 98304 | tf_op jit(solution)/shard_map/psum | solution.py:98
  37.0 1.0 copy.35
  38.0 0.8 constant_dynamic-slice_fusion.1
  38.8 1.1 fusion.21
  39.9 0.8 pad_maximum_fusion
  40.7 0.0 all-gather.3.cloned.1.call-update
  40.7 0.0 all-gather.5.cloned.1.call-start
  40.8 1.0 copy.38
  41.8 1.1 fusion.22
  42.9 0.8 pad_maximum_fusion.1
  43.6 0.0 all-gather.5.cloned.1.call-update
  43.7 1.2 dynamic_slice.38
  45.5 0.6 add_reduce_fusion
  46.1 1.1 copy.40
  47.2 0.8 select_reduce_fusion
  48.1 29.3 %all-gather.3.cloned.1.call-done = bf16[3072,2,128]{2,0,1:T(8,128)(2,1)} async-done(((bf16[768,2,128]{2,0,1:T(8,128)(2,1)}), bf16[3072,2,128]{2,0,1:T(8,128)(2,1)}) %all-gather.3.cloned.1.call-update) | async-done | bytes 1572880 | tf_op jit(solution)/shard_map/all_gather | solution.py:119
  77.4 1.5 copy.39
  78.9 36.0 %all-gather.5.cloned.1.call-done = bf16[3072,2,128]{2,0,1:T(8,128)(2,1)} async-done(((bf16[768,2,128]{2,0,1:T(8,128)(2,1)}), bf16[3072,2,128]{2,0,1:T(8,128)(2,1)}) %all-gather.5.cloned.1.call-update) | async-done | bytes 1572880 | tf_op jit(solution)/shard_map/all_gather | solution.py:120
  114.9 2.7 %copy.41 = bf16[3,1024,2,128]{3,1,2,0:T(8,128)(2,1)} copy(bf16[3,1024,2,128]{3,1,0,2:T(8,128)(2,1)} %bitcast.83) | data formatting | bytes 3145728
  117.6 1.0 broadcast_in_dim.56
  118.6 31.8 %while.15 = (s32[]{:T(128)}, f32[2,4,256]{2,1,0:T(4,128)S(1)}, f32[2,4,256]{2,1,0:T(4,128)S(1)}, f32[2,4,256,128]{3,2,1,0:T(8,128)}, s32[3,1024]{1,0:T(4,128)S(1...) while((s32[]{:T(128)}, f32[2,4,256]{2,1,0:T(4,128)S(1)}, ...), condition=%wide.region_9.10_spmd.clone, body=%wide.region_3.9_spmd.clone.sunk | while | flops 1101796608 | bytes 38421312 | solution.py:69
  118.6 0.6 fusion.45
  120.5 8.7 %conditional.3 = (f32[2,4,256]{2,1,0:T(4,128)S(1)}, f32[2,4,256]{2,1,0:T(4,128)S(1)}, f32[2,4,256,128]{3,2,1,0:T(8,128)}) conditional(s32[]{:T(128)} %convert_element_type.57, (s32[1,1024]{1,0:T(1,128)S(1)}, s32[]{:T(128)}, bf16[3,1024,2,128]{3,1,2,0:T(8,128)(2,1)S(1)}, s32[]{:T(128)}, bf16[256,2,4,128]{3,0,2,1:T(8,128)(2,1)S(1)}, ...), branch_computations={%region_5.7_spmd, %region_8.8_spmd} | conditional | flops 1101795584 | bytes 38395480 | solution.py:67
  120.5 0.2 broadcast_compare_fusion
  120.7 0.0 copy-start.1
  120.7 1.4 fusion.2
  122.2 2.0 %fusion.4 = f32[2,4,256]{2,1,0:T(4,128)S(1)} fusion(f32[2,1024,256,4]{2,1,3,0:T(8,128)S(1)} %get-tuple-element.228, f32[2,4,256]{2,1,0:T(4,128)S(1)} %max.4, pred[256,1024]{0,1:T(8,128)(4,1)S(1)} %broadcast_compare_fusion), kind=kLoop, calls=%fused_computation.5 | loop fusion | flops 10483712 | bytes 8667136 | tf_op jit(solution)/shard_map/while/body/eval_jaxpr/cond/branch_0_fun/reduce_sum | solution.py:57
  124.2 0.0 copy-done.1
  124.2 4.0 %fusion.8 = f32[2,4,256,128]{3,2,1,0:T(8,128)S(1)} fusion(f32[2,1024,256,4]{2,1,3,0:T(8,128)S(1)} %get-tuple-element.228, f32[2,4,256]{2,1,0:T(4,128)S(1)} %max.4, pred[256,1024]{0,1:T(8,128)(4,1)S(1)} %broadcast_compare_fusion, f32[2,4,256,128]{3,2,1,0:T(8,128)S(1)} %copy-done.1, bf16[3,1024,2,128]{3,1,2,0:T(8,128)(2,1)} %get-tuple-element.125, ...), kind=kOutput, calls=%fused_computation.8 | convolution fusion | flops 547880960 | bytes 11289088 | tf_op jit(solution)/shard_map/while/body/eval_jaxpr/cond/branch_0_fun/kgts,skd->kgtd/dot_general | solution.py:58
  128.3 0.0 copy-start.2
  128.3 1.0 copy-done.2
  129.2 0.6 fusion.45
  131.1 8.7 %conditional.3 = (f32[2,4,256]{2,1,0:T(4,128)S(1)}, f32[2,4,256]{2,1,0:T(4,128)S(1)}, f32[2,4,256,128]{3,2,1,0:T(8,128)}) conditional(s32[]{:T(128)} %convert_element_type.57, (s32[1,1024]{1,0:T(1,128)S(1)}, s32[]{:T(128)}, bf16[3,1024,2,128]{3,1,2,0:T(8,128)(2,1)S(1)}, s32[]{:T(128)}, bf16[256,2,4,128]{3,0,2,1:T(8,128)(2,1)S(1)}, ...), branch_computations={%region_5.7_spmd, %region_8.8_spmd} | conditional | flops 1101795584 | bytes 38395480 | solution.py:67
  131.1 0.2 broadcast_compare_fusion
  131.3 0.0 copy-start.1
  131.3 1.4 fusion.2
  132.8 2.0 %fusion.4 = f32[2,4,256]{2,1,0:T(4,128)S(1)} fusion(f32[2,1024,256,4]{2,1,3,0:T(8,128)S(1)} %get-tuple-element.228, f32[2,4,256]{2,1,0:T(4,128)S(1)} %max.4, pred[256,1024]{0,1:T(8,128)(4,1)S(1)} %broadcast_compare_fusion), kind=kLoop, calls=%fused_computation.5 | loop fusion | flops 10483712 | bytes 8667136 | tf_op jit(solution)/shard_map/while/body/eval_jaxpr/cond/branch_0_fun/reduce_sum | solution.py:57
  134.8 0.0 copy-done.1
  134.8 4.0 %fusion.8 = f32[2,4,256,128]{3,2,1,0:T(8,128)S(1)} fusion(f32[2,1024,256,4]{2,1,3,0:T(8,128)S(1)} %get-tuple-element.228, f32[2,4,256]{2,1,0:T(4,128)S(1)} %max.4, pred[256,1024]{0,1:T(8,128)(4,1)S(1)} %broadcast_compare_fusion, f32[2,4,256,128]{3,2,1,0:T(8,128)S(1)} %copy-done.1, bf16[3,1024,2,128]{3,1,2,0:T(8,128)(2,1)} %get-tuple-element.125, ...), kind=kOutput, calls=%fused_computation.8 | convolution fusion | flops 547880960 | bytes 11289088 | tf_op jit(solution)/shard_map/while/body/eval_jaxpr/cond/branch_0_fun/kgts,skd->kgtd/dot_general | solution.py:58
  138.9 0.0 copy-start.2
  138.9 1.0 copy-done.2
  139.8 0.6 fusion.45
  141.7 8.7 %conditional.3 = (f32[2,4,256]{2,1,0:T(4,128)S(1)}, f32[2,4,256]{2,1,0:T(4,128)S(1)}, f32[2,4,256,128]{3,2,1,0:T(8,128)}) conditional(s32[]{:T(128)} %convert_element_type.57, (s32[1,1024]{1,0:T(1,128)S(1)}, s32[]{:T(128)}, bf16[3,1024,2,128]{3,1,2,0:T(8,128)(2,1)S(1)}, s32[]{:T(128)}, bf16[256,2,4,128]{3,0,2,1:T(8,128)(2,1)S(1)}, ...), branch_computations={%region_5.7_spmd, %region_8.8_spmd} | conditional | flops 1101795584 | bytes 38395480 | solution.py:67
  141.7 0.2 broadcast_compare_fusion
  141.9 0.0 copy-start.1
  141.9 1.4 fusion.2
  143.4 2.0 %fusion.4 = f32[2,4,256]{2,1,0:T(4,128)S(1)} fusion(f32[2,1024,256,4]{2,1,3,0:T(8,128)S(1)} %get-tuple-element.228, f32[2,4,256]{2,1,0:T(4,128)S(1)} %max.4, pred[256,1024]{0,1:T(8,128)(4,1)S(1)} %broadcast_compare_fusion), kind=kLoop, calls=%fused_computation.5 | loop fusion | flops 10483712 | bytes 8667136 | tf_op jit(solution)/shard_map/while/body/eval_jaxpr/cond/branch_0_fun/reduce_sum | solution.py:57
  145.4 0.0 copy-done.1
  145.4 4.0 %fusion.8 = f32[2,4,256,128]{3,2,1,0:T(8,128)S(1)} fusion(f32[2,1024,256,4]{2,1,3,0:T(8,128)S(1)} %get-tuple-element.228, f32[2,4,256]{2,1,0:T(4,128)S(1)} %max.4, pred[256,1024]{0,1:T(8,128)(4,1)S(1)} %broadcast_compare_fusion, f32[2,4,256,128]{3,2,1,0:T(8,128)S(1)} %copy-done.1, bf16[3,1024,2,128]{3,1,2,0:T(8,128)(2,1)} %get-tuple-element.125, ...), kind=kOutput, calls=%fused_computation.8 | convolution fusion | flops 547880960 | bytes 11289088 | tf_op jit(solution)/shard_map/while/body/eval_jaxpr/cond/branch_0_fun/kgts,skd->kgtd/dot_general | solution.py:58
  149.5 0.0 copy-start.2
  149.5 1.0 copy-done.2
  150.4 0.2 copy.42
  150.6 2.9 %fusion.24 = bf16[256,2,4,128]{3,2,1,0:T(4,128)(2,1)} fusion(f32[2,4,256]{1,0,2:T(2,128)S(1)} %copy.42, f32[2,4,256,128]{3,2,1,0:T(8,128)} %get-tuple-element.142), kind=kLoop, calls=%fused_computation.31 | loop fusion | flops 524288 | bytes 1581056 | tf_op jit(solution)/shard_map/convert_element_type | solution.py:128
  (21 shorter events, 0.1 us)
Async XLA Ops:
  6.5 3.2 %copy-start = (bf16[256,1024]{1,0:T(8,128)(2,1)S(1)}, bf16[256,1024]{1,0:T(8,128)(2,1)}, u32[]{:S(2)}) copy-start(bf16[256,1024]{1,0:T(8,128)(2,1)} %param.16) | copy-start | bytes 1572868
  6.5 70.8 %all-gather.3.cloned.1.call-start = ((), (), s32[]{:S(2)}) async-start(), calls=%async_computation | async-start | bytes 1966080 | tf_op jit(solution)/shard_map/all_gather | solution.py:119
  40.7 74.2 %all-gather.5.cloned.1.call-start = ((), (), s32[]{:S(2)}) async-start(), calls=%async_computation.1 | async-start | bytes 1966080 | tf_op jit(solution)/shard_map/all_gather | solution.py:120
  120.7 3.5 %copy-start.1 = (f32[2,4,256,128]{3,2,1,0:T(8,128)S(1)}, f32[2,4,256,128]{3,2,1,0:T(8,128)}, u32[]{:S(2)}) copy-start(f32[2,4,256,128]{3,2,1,0:T(8,128)} %get-tuple-element.124) | copy-start | bytes 3145732 | tf_op jit(solution)/shard_map/while/body/eval_jaxpr/cond
  128.3 1.0 copy-start.2
  131.3 3.5 %copy-start.1 = (f32[2,4,256,128]{3,2,1,0:T(8,128)S(1)}, f32[2,4,256,128]{3,2,1,0:T(8,128)}, u32[]{:S(2)}) copy-start(f32[2,4,256,128]{3,2,1,0:T(8,128)} %get-tuple-element.124) | copy-start | bytes 3145732 | tf_op jit(solution)/shard_map/while/body/eval_jaxpr/cond
  138.9 1.0 copy-start.2
  141.9 3.5 %copy-start.1 = (f32[2,4,256,128]{3,2,1,0:T(8,128)S(1)}, f32[2,4,256,128]{3,2,1,0:T(8,128)}, u32[]{:S(2)}) copy-start(f32[2,4,256,128]{3,2,1,0:T(8,128)} %get-tuple-element.124) | copy-start | bytes 3145732 | tf_op jit(solution)/shard_map/while/body/eval_jaxpr/cond
  149.5 1.0 copy-start.2
Sparse Core Ops, SparseCore 0:
  40.8 36.4 all-gather.2
  78.9 35.9 all-gather.4
where the time goes:
time: 161 us; the launch traced here: 160 us
  waiting for transfers between devices  65.4 us (41%)
  blocking collectives  26 us (16%)
  matrix products  19.7 us (12%)
  between operations  16 us (10%)
  local copies, waits for them, and re-layouts  14.8 us (9%)
  other arithmetic  14.6 us (9%)
  loops' own time  3.9 us (2%)
    all_gather x1, waiting for transfers between devices, on_device(): value_piece = lax.all_gather(value_rows, 'blk', axis=0, tiled=True)  36 us
    all_gather x1, waiting for transfers between devices, on_device(): key_piece = lax.all_gather(key_rows, 'blk', axis=0, tiled=True)  29.3 us
    psum x1, blocking collectives, on_device(): latent = lax.psum(partial_latent, ('team', 'head')).astype(jnp.bfloat16)  26 us
    dot_general x3, matrix products, compute(): jnp.einsum('kgts,skd->kgtd', weights.astype(jnp.bfloat16), block_values,...  12.1 us
    unnamed x7, local copies, waits for them, and re-layouts  7.28 us
    reduce_sum x3, other arithmetic, compute(): row_sum = row_sum * factor + jnp.sum(weights, axis=-1)  6.09 us
    dot_general x3, matrix products, compute(): jnp.einsum('tkgd,skd->kgts', query_rows, block_keys, preferred_element_ty...  4.2 us
    another operation x1, loops' own time, attend(): result, _ = lax.scan(advance, running, (key_split, value_split, pos_split))  3.67 us
  transfers between devices with their start and end apart: 2, of which 2 were waited for; matrix products, arithmetic and copies ran while one was open for 5% of the time, Pallas kernels for 0%

commit v1 on v0

--- a/solution.py
+++ b/solution.py
@@ -95,7 +95,7 @@
     chosen = adapter_ids[my_block]
     down_rows = lax.dynamic_index_in_dim(adapter_down, chosen, 0, keepdims=False)
     partial_latent = jnp.dot(features, down_rows, preferred_element_type=jnp.float32)
-    latent = lax.psum(partial_latent, ("team", "head")).astype(jnp.bfloat16)
+    latent = jnp.sum(lax.all_gather(partial_latent, ("team", "head")), axis=0).astype(jnp.bfloat16)
 
     def expand(up_table, base_rows):
         up_rows = lax.dynamic_index_in_dim(up_table, chosen, 0, keepdims=False).reshape(

time: 161 us -> 148 us (0.919)
  blocking collectives: 26 us -> 11.3 us
    psum x1 -> x0, blocking collectives: 26 us -> none  [on_device(): latent = lax.psum(partial_latent, ('team', 'head')).astype(jnp.bfloat16)]
    all_gather x0 -> x1, blocking collectives: none -> 11.3 us  [on_device(): lax.all_gather(partial_latent, ('team', 'head'))]
    unnamed x7 -> x8, local copies, waits for them, and re-layouts: 7.28 us -> 7.42 us
  transfers between devices with their start and end apart: 2 -> 2, of which waited for: 2 -> 2; matrix products, arithmetic and copies ran while one was open for 5% -> 6% of each run, Pallas kernels for 0% -> 0%
where the time goes in v1:
time: 148 us; the launch traced here: 147 us
  waiting for transfers between devices  66.1 us (45%)
  matrix products  19.7 us (13%)
  between operations  16 us (11%)
  local copies, waits for them, and re-layouts  14.9 us (10%)
  other arithmetic  14.8 us (10%)
  blocking collectives  11.3 us (8%)
  loops' own time  3.9 us (3%)
    all_gather x1, waiting for transfers between devices, on_device(): value_piece = lax.all_gather(value_rows, 'blk', axis=0, tiled=True)  36 us
    all_gather x1, waiting for transfers between devices, on_device(): key_piece = lax.all_gather(key_rows, 'blk', axis=0, tiled=True)  30.1 us
    dot_general x3, matrix products, compute(): jnp.einsum('kgts,skd->kgtd', weights.astype(jnp.bfloat16), block_values,...  12.1 us
    all_gather x1, blocking collectives, on_device(): lax.all_gather(partial_latent, ('team', 'head'))  11.3 us
    unnamed x8, local copies, waits for them, and re-layouts  7.42 us
    reduce_sum x3, other arithmetic, compute(): row_sum = row_sum * factor + jnp.sum(weights, axis=-1)  6.09 us
    dot_general x3, matrix products, compute(): jnp.einsum('tkgd,skd->kgts', query_rows, block_keys, preferred_element_ty...  4.21 us
    another operation x1, loops' own time, attend(): result, _ = lax.scan(advance, running, (key_split, value_split, pos_split))  3.67 us
  transfers between devices with their start and end apart: 2, of which 2 were waited for; matrix products, arithmetic and copies ran while one was open for 6% of the time, Pallas kernels for 0%

profile of v1, /device:TPU:0, one launch (start us, length us, event | category | flops | bytes accessed | tf_op | source)
XLA Modules:
  0.0 146.8 jit_solution(10345011272907751840)
XLA Ops:
  6.5 0.0 copy-start
  6.5 0.0 all-gather.4.cloned.1.call-start
  6.5 1.3 dynamic_slice.39
  9.8 0.0 copy-done
  9.8 1.2 convolution_bitcast_fusion
  11.0 11.3 %all-gather = f32[2048,64]{0,1:T(8,128)S(1)} all-gather(f32[256,64]{0,1:T(8,128)S(1)} %convolution_bitcast_fusion), channel_id=2, replica_groups=mesh['team'=2,'blk'=4,'head'=4] {'team','head'}, dimensions={0}, use_global_device_ids=true | all-gather | bytes 589824 | tf_op jit(solution)/shard_map/all_gather | solution.py:98
  22.3 0.2 copy.49
  22.5 0.1 bitcast_reduce_fusion
  22.6 1.0 copy.35
  23.6 0.8 constant_dynamic-slice_fusion.1
  24.4 1.1 fusion.21
  25.6 0.8 pad_maximum_fusion
  26.3 0.0 all-gather.4.cloned.1.call-update
  26.4 0.0 all-gather.6.cloned.1.call-start
  26.4 1.0 copy.38
  27.4 1.1 fusion.22
  28.5 0.8 pad_maximum_fusion.1
  29.3 0.0 all-gather.6.cloned.1.call-update
  29.3 1.2 dynamic_slice.38
  31.1 0.6 add_reduce_fusion
  31.7 1.1 copy.40
  32.9 0.8 select_reduce_fusion
  33.7 30.1 %all-gather.4.cloned.1.call-done = bf16[3072,2,128]{2,0,1:T(8,128)(2,1)} async-done(((bf16[768,2,128]{2,0,1:T(8,128)(2,1)}), bf16[3072,2,128]{2,0,1:T(8,128)(2,1)}) %all-gather.4.cloned.1.call-update) | async-done | bytes 1572880 | tf_op jit(solution)/shard_map/all_gather | solution.py:119
  63.8 1.5 %copy.39 = bf16[3,1024,2,128]{3,1,2,0:T(8,128)(2,1)S(1)} copy(bf16[3,1024,2,128]{3,1,0,2:T(8,128)(2,1)} %bitcast.88) | data formatting | bytes 3145728
  65.4 36.0 %all-gather.6.cloned.1.call-done = bf16[3072,2,128]{2,0,1:T(8,128)(2,1)} async-done(((bf16[768,2,128]{2,0,1:T(8,128)(2,1)}), bf16[3072,2,128]{2,0,1:T(8,128)(2,1)}) %all-gather.6.cloned.1.call-update) | async-done | bytes 1572880 | tf_op jit(solution)/shard_map/all_gather | solution.py:120
  101.3 2.7 %copy.41 = bf16[3,1024,2,128]{3,1,2,0:T(8,128)(2,1)} copy(bf16[3,1024,2,128]{3,1,0,2:T(8,128)(2,1)} %bitcast.89) | data formatting | bytes 3145728
  104.0 1.0 broadcast_in_dim.56
  105.0 31.8 %while.15 = (s32[]{:T(128)}, f32[2,4,256]{2,1,0:T(4,128)S(1)}, f32[2,4,256]{2,1,0:T(4,128)S(1)}, f32[2,4,256,128]{3,2,1,0:T(8,128)}, s32[3,1024]{1,0:T(4,128)S(1...) while((s32[]{:T(128)}, f32[2,4,256]{2,1,0:T(4,128)S(1)}, ...), condition=%wide.region_9.10_spmd.clone, body=%wide.region_3.9_spmd.clone.sunk | while | flops 1101796608 | bytes 38421312 | solution.py:69
  105.0 0.6 fusion.45
  106.9 8.7 %conditional.3 = (f32[2,4,256]{2,1,0:T(4,128)S(1)}, f32[2,4,256]{2,1,0:T(4,128)S(1)}, f32[2,4,256,128]{3,2,1,0:T(8,128)}) conditional(s32[]{:T(128)} %convert_element_type.57, (s32[1,1024]{1,0:T(1,128)S(1)}, s32[]{:T(128)}, bf16[3,1024,2,128]{3,1,2,0:T(8,128)(2,1)S(1)}, s32[]{:T(128)}, bf16[256,2,4,128]{3,0,2,1:T(8,128)(2,1)S(1)}, ...), branch_computations={%region_5.7_spmd, %region_8.8_spmd} | conditional | flops 1101795584 | bytes 38395480 | solution.py:67
  106.9 0.2 broadcast_compare_fusion
  107.1 0.0 copy-start.1
  107.2 1.4 fusion.2
  108.6 2.0 %fusion.4 = f32[2,4,256]{2,1,0:T(4,128)S(1)} fusion(f32[2,1024,256,4]{2,1,3,0:T(8,128)S(1)} %get-tuple-element.228, f32[2,4,256]{2,1,0:T(4,128)S(1)} %max.4, pred[256,1024]{0,1:T(8,128)(4,1)S(1)} %broadcast_compare_fusion), kind=kLoop, calls=%fused_computation.5 | loop fusion | flops 10483712 | bytes 8667136 | tf_op jit(solution)/shard_map/while/body/eval_jaxpr/cond/branch_0_fun/reduce_sum | solution.py:57
  110.6 0.0 copy-done.1
  110.6 4.0 %fusion.8 = f32[2,4,256,128]{3,2,1,0:T(8,128)S(1)} fusion(f32[2,1024,256,4]{2,1,3,0:T(8,128)S(1)} %get-tuple-element.228, f32[2,4,256]{2,1,0:T(4,128)S(1)} %max.4, pred[256,1024]{0,1:T(8,128)(4,1)S(1)} %broadcast_compare_fusion, f32[2,4,256,128]{3,2,1,0:T(8,128)S(1)} %copy-done.1, bf16[3,1024,2,128]{3,1,2,0:T(8,128)(2,1)} %get-tuple-element.125, ...), kind=kOutput, calls=%fused_computation.8 | convolution fusion | flops 547880960 | bytes 11289088 | tf_op jit(solution)/shard_map/while/body/eval_jaxpr/cond/branch_0_fun/kgts,skd->kgtd/dot_general | solution.py:58
  114.7 0.0 copy-start.2
  114.7 1.0 copy-done.2
  115.6 0.6 fusion.45
  117.5 8.7 %conditional.3 = (f32[2,4,256]{2,1,0:T(4,128)S(1)}, f32[2,4,256]{2,1,0:T(4,128)S(1)}, f32[2,4,256,128]{3,2,1,0:T(8,128)}) conditional(s32[]{:T(128)} %convert_element_type.57, (s32[1,1024]{1,0:T(1,128)S(1)}, s32[]{:T(128)}, bf16[3,1024,2,128]{3,1,2,0:T(8,128)(2,1)S(1)}, s32[]{:T(128)}, bf16[256,2,4,128]{3,0,2,1:T(8,128)(2,1)S(1)}, ...), branch_computations={%region_5.7_spmd, %region_8.8_spmd} | conditional | flops 1101795584 | bytes 38395480 | solution.py:67
  117.5 0.2 broadcast_compare_fusion
  117.7 0.0 copy-start.1
  117.8 1.4 fusion.2
  119.2 2.0 %fusion.4 = f32[2,4,256]{2,1,0:T(4,128)S(1)} fusion(f32[2,1024,256,4]{2,1,3,0:T(8,128)S(1)} %get-tuple-element.228, f32[2,4,256]{2,1,0:T(4,128)S(1)} %max.4, pred[256,1024]{0,1:T(8,128)(4,1)S(1)} %broadcast_compare_fusion), kind=kLoop, calls=%fused_computation.5 | loop fusion | flops 10483712 | bytes 8667136 | tf_op jit(solution)/shard_map/while/body/eval_jaxpr/cond/branch_0_fun/reduce_sum | solution.py:57
  121.2 0.0 copy-done.1
  121.2 4.0 %fusion.8 = f32[2,4,256,128]{3,2,1,0:T(8,128)S(1)} fusion(f32[2,1024,256,4]{2,1,3,0:T(8,128)S(1)} %get-tuple-element.228, f32[2,4,256]{2,1,0:T(4,128)S(1)} %max.4, pred[256,1024]{0,1:T(8,128)(4,1)S(1)} %broadcast_compare_fusion, f32[2,4,256,128]{3,2,1,0:T(8,128)S(1)} %copy-done.1, bf16[3,1024,2,128]{3,1,2,0:T(8,128)(2,1)} %get-tuple-element.125, ...), kind=kOutput, calls=%fused_computation.8 | convolution fusion | flops 547880960 | bytes 11289088 | tf_op jit(solution)/shard_map/while/body/eval_jaxpr/cond/branch_0_fun/kgts,skd->kgtd/dot_general | solution.py:58
  125.3 0.0 copy-start.2
  125.3 1.0 copy-done.2
  126.2 0.6 fusion.45
  128.1 8.7 %conditional.3 = (f32[2,4,256]{2,1,0:T(4,128)S(1)}, f32[2,4,256]{2,1,0:T(4,128)S(1)}, f32[2,4,256,128]{3,2,1,0:T(8,128)}) conditional(s32[]{:T(128)} %convert_element_type.57, (s32[1,1024]{1,0:T(1,128)S(1)}, s32[]{:T(128)}, bf16[3,1024,2,128]{3,1,2,0:T(8,128)(2,1)S(1)}, s32[]{:T(128)}, bf16[256,2,4,128]{3,0,2,1:T(8,128)(2,1)S(1)}, ...), branch_computations={%region_5.7_spmd, %region_8.8_spmd} | conditional | flops 1101795584 | bytes 38395480 | solution.py:67
  128.1 0.2 broadcast_compare_fusion
  128.4 0.0 copy-start.1
  128.4 1.4 fusion.2
  129.8 2.0 %fusion.4 = f32[2,4,256]{2,1,0:T(4,128)S(1)} fusion(f32[2,1024,256,4]{2,1,3,0:T(8,128)S(1)} %get-tuple-element.228, f32[2,4,256]{2,1,0:T(4,128)S(1)} %max.4, pred[256,1024]{0,1:T(8,128)(4,1)S(1)} %broadcast_compare_fusion), kind=kLoop, calls=%fused_computation.5 | loop fusion | flops 10483712 | bytes 8667136 | tf_op jit(solution)/shard_map/while/body/eval_jaxpr/cond/branch_0_fun/reduce_sum | solution.py:57
  131.8 0.0 copy-done.1
  131.8 4.0 %fusion.8 = f32[2,4,256,128]{3,2,1,0:T(8,128)S(1)} fusion(f32[2,1024,256,4]{2,1,3,0:T(8,128)S(1)} %get-tuple-element.228, f32[2,4,256]{2,1,0:T(4,128)S(1)} %max.4, pred[256,1024]{0,1:T(8,128)(4,1)S(1)} %broadcast_compare_fusion, f32[2,4,256,128]{3,2,1,0:T(8,128)S(1)} %copy-done.1, bf16[3,1024,2,128]{3,1,2,0:T(8,128)(2,1)} %get-tuple-element.125, ...), kind=kOutput, calls=%fused_computation.8 | convolution fusion | flops 547880960 | bytes 11289088 | tf_op jit(solution)/shard_map/while/body/eval_jaxpr/cond/branch_0_fun/kgts,skd->kgtd/dot_general | solution.py:58
  135.9 0.0 copy-start.2
  135.9 1.0 copy-done.2
  136.8 0.2 copy.42
  137.0 2.9 %fusion.24 = bf16[256,2,4,128]{3,2,1,0:T(4,128)(2,1)} fusion(f32[2,4,256]{1,0,2:T(2,128)S(1)} %copy.42, f32[2,4,256,128]{3,2,1,0:T(8,128)} %get-tuple-element.142), kind=kLoop, calls=%fused_computation.32 | loop fusion | flops 524288 | bytes 1581056 | tf_op jit(solution)/shard_map/convert_element_type | solution.py:128
  (21 shorter events, 0.1 us)
Async XLA Ops:
  6.5 3.2 %copy-start = (bf16[256,1024]{1,0:T(8,128)(2,1)S(1)}, bf16[256,1024]{1,0:T(8,128)(2,1)}, u32[]{:S(2)}) copy-start(bf16[256,1024]{1,0:T(8,128)(2,1)} %param.16) | copy-start | bytes 1572868
  6.5 57.3 %all-gather.4.cloned.1.call-start = ((), (), s32[]{:S(2)}) async-start(), calls=%async_computation | async-start | bytes 1966080 | tf_op jit(solution)/shard_map/all_gather | solution.py:119
  26.4 75.0 %all-gather.6.cloned.1.call-start = ((), (), s32[]{:S(2)}) async-start(), calls=%async_computation.1 | async-start | bytes 1966080 | tf_op jit(solution)/shard_map/all_gather | solution.py:120
  107.1 3.5 %copy-start.1 = (f32[2,4,256,128]{3,2,1,0:T(8,128)S(1)}, f32[2,4,256,128]{3,2,1,0:T(8,128)}, u32[]{:S(2)}) copy-start(f32[2,4,256,128]{3,2,1,0:T(8,128)} %get-tuple-element.124) | copy-start | bytes 3145732 | tf_op jit(solution)/shard_map/while/body/eval_jaxpr/cond
  114.7 1.0 copy-start.2
  117.7 3.5 %copy-start.1 = (f32[2,4,256,128]{3,2,1,0:T(8,128)S(1)}, f32[2,4,256,128]{3,2,1,0:T(8,128)}, u32[]{:S(2)}) copy-start(f32[2,4,256,128]{3,2,1,0:T(8,128)} %get-tuple-element.124) | copy-start | bytes 3145732 | tf_op jit(solution)/shard_map/while/body/eval_jaxpr/cond
  125.3 1.0 copy-start.2
  128.4 3.5 %copy-start.1 = (f32[2,4,256,128]{3,2,1,0:T(8,128)S(1)}, f32[2,4,256,128]{3,2,1,0:T(8,128)}, u32[]{:S(2)}) copy-start(f32[2,4,256,128]{3,2,1,0:T(8,128)} %get-tuple-element.124) | copy-start | bytes 3145732 | tf_op jit(solution)/shard_map/while/body/eval_jaxpr/cond
  135.9 1.0 copy-start.2
Sparse Core Ops, SparseCore 0:
  26.5 37.3 all-gather.3
  65.4 35.8 all-gather.5
